TPU v7x, 32 devices: a whole 2x2x4 slice. The times are simulated.
32 devices in a mesh: fsdp: 4 (over y, x), ctx: 4 (over z), tp: 2 (over core).
Axes of the slice: x: 2, y: 2, z: 4, core: 2. Of those that a mesh axis runs over, the one named last changes fastest.
Arguments:
- tokens: bfloat16 [8, 1024, 2048], P('fsdp', 'ctx'), may hold values from -6 to 6
- cotangent: bfloat16 [8, 1024, 2048], P('fsdp', 'ctx'), may hold values from -6 to 6
- prefix_len: int32 [8], P('fsdp'), may hold values from 102 to 512
- group_order: int32 [8], replicated, may hold values from 0 to 7, each once
- ln_gain: bfloat16 [2048], replicated, may hold values from 0.25 to 1.75
- ln_bias: bfloat16 [2048], replicated, may hold values from -4 to 4
- query_weight: bfloat16 [2048, 2048], P('fsdp', 'tp'), may hold values from -0.125 to 0.125
- query_bias: bfloat16 [2048], P('tp'), may hold values from -4 to 4
- key_weight: bfloat16 [2048, 2048], P('fsdp', 'tp'), may hold values from -0.125 to 0.125
- key_bias: bfloat16 [2048], P('tp'), may hold values from -4 to 4
- value_weight: bfloat16 [2048, 2048], P('fsdp', 'tp'), may hold values from -0.125 to 0.125
- value_bias: bfloat16 [2048], P('tp'), may hold values from -4 to 4
- out_weight: bfloat16 [2048, 2048], P('fsdp', 'tp'), may hold values from -1 to 1
- out_bias: bfloat16 [2048], replicated, may hold values from -4 to 4
- up_weight: bfloat16 [2048, 8192], P('fsdp', 'tp'), may hold values from -0.125 to 0.125
- up_bias: bfloat16 [8192], P('tp'), may hold values from -4 to 4
- down_weight: bfloat16 [2048, 8192], P('fsdp', 'tp'), may hold values from -0.0625 to 0.0625
- down_bias: bfloat16 [2048], replicated, may hold values from -4 to 4
Outputs:
- output: bfloat16 [8, 1024, 2048], P('fsdp', 'ctx')
- input_grad: bfloat16 [8, 1024, 2048], P('fsdp', 'ctx')
- ln_gain_grad: float32 [2048], replicated
- ln_bias_grad: float32 [2048], replicated
- query_weight_grad: float32 [2048, 2048], P('fsdp', 'tp')
- query_bias_grad: float32 [2048], P('tp')
- key_weight_grad: float32 [2048, 2048], P('fsdp', 'tp')
- key_bias_grad: float32 [2048], P('tp')
- value_weight_grad: float32 [2048, 2048], P('fsdp', 'tp')
- value_bias_grad: float32 [2048], P('tp')
- out_weight_grad: float32 [2048, 2048], P('fsdp', 'tp')
- up_weight_grad: float32 [2048, 8192], P('fsdp', 'tp')
- up_bias_grad: float32 [8192], P('tp')
- down_weight_grad: float32 [2048, 8192], P('fsdp', 'tp')
- out_biases_grad: float32 [2048], replicated
Inputs may be any that keep to these rules, and one draw needn't show every extreme that they name: Each number of 0 to 7 appears once; storage rows k * 128 to k * 128 + 127 of every sequence hold positions group_order[k] * 128 onwards.
All inputs are finite; a program needn't handle non-finite values.
Results may differ from a plain program's by a relative error of at most 0.012.
Values may be sent and summed in bfloat16 or wider, within the bound.
No kernel may reach another device: no remote copies, remote signals or barrier semaphores. Data moves between devices by JAX's collectives and lax.ppermute only.
A program may use at most 448 MiB of HBM per device.

v0:
```python
import jax
import jax.numpy as jnp
from jax import lax
from jax.sharding import PartitionSpec as P

HD = 64
ROT = 32
SEQ_LEN = 1024
masked_fill = -1e30
norm_eps = 1e-05


def positions(group_order, row_start, row_count, group_len):
    row_index = row_start + jnp.arange(row_count, dtype=jnp.int32)
    slot_index = row_index // group_len
    offset = row_index - slot_index * group_len
    matches = slot_index[:, None] == jnp.arange(group_order.shape[0], dtype=jnp.int32)[None, :]
    anchor = jnp.sum(jnp.where(matches, group_order[None, :], 0), axis=1)
    return anchor * group_len + offset


def rotary_tables(places):
    half_rot = ROT // 2
    frequency = jnp.power(10000.0, -2.0 * jnp.arange(half_rot, dtype=jnp.float32) / ROT)
    angles = places.astype(jnp.float32)[:, None] * frequency[None, :]
    return (jnp.cos(angles), jnp.sin(angles))


def rotate(tensor, cosine, sine_vals):
    half_rot = cosine.shape[-1]
    front_part = tensor[..., :half_rot]
    back_part = tensor[..., half_rot : 2 * half_rot]
    rest_part = tensor[..., 2 * half_rot :]
    cosine_rows = cosine[:, None, :]
    sine_rows = sine_vals[:, None, :]
    return jnp.concatenate(
        [
            front_part * cosine_rows - back_part * sine_rows,
            back_part * cosine_rows + front_part * sine_rows,
            rest_part,
        ],
        axis=-1,
    )


def gelu_tanh(values_in):
    return jax.nn.gelu(values_in, approximate=True)


def local(
    tokens,
    cotangent,
    prefix_len,
    group_order,
    ln_gain,
    ln_bias,
    query_weight,
    query_bias,
    key_weight,
    key_bias,
    value_weight,
    value_bias,
    out_weight,
    out_bias,
    up_weight,
    up_bias,
    down_weight,
    down_bias,
):
    seq_count, local_rows, model_width = tokens.shape
    token_count = seq_count * local_rows
    inner_width = query_weight.shape[1]
    local_heads = inner_width // HD
    hidden_units = up_weight.shape[1]
    group_len = SEQ_LEN // group_order.shape[0]
    score_scale = HD ** (-0.5)
    own_place = positions(group_order, lax.axis_index("ctx") * local_rows, local_rows, group_len)
    key_place = positions(group_order, 0, SEQ_LEN, group_len)
    cosine, sine_vals = rotary_tables(own_place)
    allowed = (key_place[None, None, None, :] <= own_place[None, None, :, None]) | (
        key_place[None, None, None, :] < prefix_len[:, None, None, None]
    )
    gathered = (
        lax.all_gather(query_weight, "fsdp", axis=0, tiled=True),
        lax.all_gather(key_weight, "fsdp", axis=0, tiled=True),
        lax.all_gather(value_weight, "fsdp", axis=0, tiled=True),
        lax.all_gather(out_weight, "fsdp", axis=0, tiled=True),
        lax.all_gather(up_weight, "fsdp", axis=0, tiled=True),
        lax.all_gather(down_weight, "fsdp", axis=0, tiled=True),
    )
    w_query, w_key, w_value, w_out, w_up, w_down = gathered
    inputs = tokens.reshape(token_count, model_width).astype(jnp.float32)
    centre = jnp.mean(inputs, axis=-1, keepdims=True)
    centred = inputs - centre
    inv_std = lax.rsqrt(jnp.mean(centred * centred, axis=-1, keepdims=True) + norm_eps)
    normed = centred * inv_std
    norm_gain = ln_gain.astype(jnp.float32)
    hidden = (normed * norm_gain + ln_bias.astype(jnp.float32)).astype(jnp.bfloat16)

    def project(weight, bias_vec):
        return jnp.dot(hidden, weight, preferred_element_type=jnp.float32) + bias_vec.astype(
            jnp.float32
        )

    query_rot = rotate(
        project(w_query, query_bias).reshape(seq_count, local_rows, local_heads, HD),
        cosine,
        sine_vals,
    ).astype(jnp.bfloat16)
    key_rot = (
        rotate(
            project(w_key, key_bias).reshape(seq_count, local_rows, local_heads, HD),
            cosine,
            sine_vals,
        )
        .astype(jnp.bfloat16)
        .reshape(seq_count, local_rows, inner_width)
    )
    value_rows = (
        project(w_value, value_bias)
        .astype(jnp.bfloat16)
        .reshape(seq_count, local_rows, inner_width)
    )
    keys_all, values_all = (
        lax.all_gather(key_rot, "ctx", axis=1, tiled=True),
        lax.all_gather(value_rows, "ctx", axis=1, tiled=True),
    )

    def scores_for(key_block):
        key_heads = key_block.reshape(seq_count, key_block.shape[1], local_heads, HD)
        raw_scores = (
            jnp.einsum("bqhd,bkhd->bhqk", query_rot, key_heads, preferred_element_type=jnp.float32)
            * score_scale
        )
        return jnp.where(allowed, raw_scores, masked_fill)

    masked = scores_for(keys_all)
    row_max = jnp.max(masked, axis=-1, keepdims=True)
    exponent = jnp.exp(masked - row_max)
    row_total = jnp.sum(exponent, axis=-1, keepdims=True)
    attn_probs = (exponent / row_total).astype(jnp.bfloat16)
    log_total = row_max + jnp.log(row_total)
    value_heads = values_all.reshape(seq_count, values_all.shape[1], local_heads, HD)
    context = jnp.einsum(
        "bhqk,bkhd->bqhd", attn_probs, value_heads, preferred_element_type=jnp.float32
    )
    context = context.reshape(token_count, inner_width).astype(jnp.bfloat16)
    up_proj = project(w_up, up_bias)
    activated = gelu_tanh(up_proj).astype(jnp.bfloat16)
    partial_out = jnp.dot(context, w_out.T, preferred_element_type=jnp.float32) + jnp.dot(
        activated, w_down.T, preferred_element_type=jnp.float32
    )
    branches = lax.psum(partial_out, "tp")
    output = inputs + branches + out_bias.astype(jnp.float32) + down_bias.astype(jnp.float32)
    output = output.astype(jnp.bfloat16).reshape(seq_count, local_rows, model_width)
    back_query, back_key, back_value, back_out, back_up, back_down = (
        lax.all_gather(query_weight, "fsdp", axis=0, tiled=True),
        lax.all_gather(key_weight, "fsdp", axis=0, tiled=True),
        lax.all_gather(value_weight, "fsdp", axis=0, tiled=True),
        lax.all_gather(out_weight, "fsdp", axis=0, tiled=True),
        lax.all_gather(up_weight, "fsdp", axis=0, tiled=True),
        lax.all_gather(down_weight, "fsdp", axis=0, tiled=True),
    )
    keys_back, values_back = (
        lax.all_gather(key_rot, "ctx", axis=1, tiled=True),
        lax.all_gather(value_rows, "ctx", axis=1, tiled=True),
    )
    grad_out = cotangent.reshape(token_count, model_width)
    grad_context = jnp.dot(grad_out, back_out, preferred_element_type=jnp.float32).astype(
        jnp.bfloat16
    )
    grad_heads = grad_context.reshape(seq_count, local_rows, local_heads, HD)
    key_heads_back = keys_back.reshape(seq_count, keys_back.shape[1], local_heads, HD)
    value_heads_back = values_back.reshape(seq_count, values_back.shape[1], local_heads, HD)
    probs_back = jnp.exp(scores_for(keys_back) - log_total)
    grad_probs = jnp.einsum(
        "bqhd,bkhd->bhqk", grad_heads, value_heads_back, preferred_element_type=jnp.float32
    )
    row_delta = jnp.sum(probs_back * grad_probs, axis=-1, keepdims=True)
    grad_scores = (probs_back * (grad_probs - row_delta)).astype(jnp.bfloat16)
    probs_low = probs_back.astype(jnp.bfloat16)
    grad_query_rot = (
        jnp.einsum(
            "bhqk,bkhd->bqhd", grad_scores, key_heads_back, preferred_element_type=jnp.float32
        )
        * score_scale
    )
    row_count = local_rows * lax.axis_size("ctx")
    grad_key_part = (
        jnp.einsum("bhqk,bqhd->kbhd", grad_scores, query_rot, preferred_element_type=jnp.float32)
        * score_scale
    )
    grad_value_part = jnp.einsum(
        "bhqk,bqhd->kbhd", probs_low, grad_heads, preferred_element_type=jnp.float32
    )
    key_grads = lax.psum_scatter(
        jnp.concatenate(
            [
                grad_key_part.reshape(row_count, seq_count, inner_width),
                grad_value_part.reshape(row_count, seq_count, inner_width),
            ],
            axis=2,
        ),
        "ctx",
        scatter_dimension=0,
        tiled=True,
    )
    key_grads = jnp.transpose(key_grads, (1, 0, 2))
    key_grad_rot = key_grads[:, :, :inner_width].reshape(seq_count, local_rows, local_heads, HD)
    grad_value = (
        key_grads[:, :, inner_width:].astype(jnp.bfloat16).reshape(token_count, inner_width)
    )
    grad_query = (
        rotate(grad_query_rot, cosine, -sine_vals)
        .astype(jnp.bfloat16)
        .reshape(token_count, inner_width)
    )
    grad_key = (
        rotate(key_grad_rot, cosine, -sine_vals)
        .astype(jnp.bfloat16)
        .reshape(token_count, inner_width)
    )
    grad_activated = jnp.dot(grad_out, back_down, preferred_element_type=jnp.float32)
    gelu_pull = jax.vjp(gelu_tanh, up_proj)[1]
    grad_up = gelu_pull(grad_activated)[0].astype(jnp.bfloat16)
    partial_hidden = (
        jnp.dot(grad_query, back_query.T, preferred_element_type=jnp.float32)
        + jnp.dot(grad_key, back_key.T, preferred_element_type=jnp.float32)
        + jnp.dot(grad_value, back_value.T, preferred_element_type=jnp.float32)
        + jnp.dot(grad_up, back_up.T, preferred_element_type=jnp.float32)
    )
    grad_hidden = lax.psum(partial_hidden, "tp")
    grad_scaled = grad_hidden * norm_gain
    grad_normed = inv_std * (
        grad_scaled
        - jnp.mean(grad_scaled, axis=-1, keepdims=True)
        - normed * jnp.mean(grad_scaled * normed, axis=-1, keepdims=True)
    )
    grad_float = grad_out.astype(jnp.float32)
    input_grad = (
        (grad_float + grad_normed).astype(jnp.bfloat16).reshape(seq_count, local_rows, model_width)
    )
    small_terms = (
        jnp.sum(grad_hidden * normed, axis=0),
        jnp.sum(grad_hidden, axis=0),
        jnp.sum(grad_query, axis=0, dtype=jnp.float32),
        jnp.sum(grad_key, axis=0, dtype=jnp.float32),
        jnp.sum(grad_value, axis=0, dtype=jnp.float32),
        jnp.sum(grad_up, axis=0, dtype=jnp.float32),
        jnp.sum(grad_float, axis=0),
    )
    gain_grad, shift_grad, qbias_grad, kbias_grad, vbias_grad, ubias_grad, obias_grad = lax.psum(
        (
            small_terms[0],
            small_terms[1],
            small_terms[2],
            small_terms[3],
            small_terms[4],
            small_terms[5],
            small_terms[6],
        ),
        ("fsdp", "ctx"),
    )
    grads_in = jnp.concatenate([grad_query, grad_key, grad_value, grad_up], axis=1)
    acts_out = jnp.concatenate([context, activated], axis=1)
    left_part = jnp.einsum("tc,tn->cn", hidden, grads_in, preferred_element_type=jnp.float32)
    right_part = jnp.einsum("tc,tn->cn", grad_out, acts_out, preferred_element_type=jnp.float32)
    scattered = lax.psum_scatter(
        jnp.concatenate([left_part, right_part], axis=1), "fsdp", scatter_dimension=0, tiled=True
    )
    weight_grads = lax.psum(scattered, "ctx")
    edge_two = 2 * inner_width
    edge_three = 3 * inner_width
    edge_four = edge_three + hidden_units
    edge_five = edge_four + inner_width
    return (
        output,
        input_grad,
        gain_grad,
        shift_grad,
        weight_grads[:, :inner_width],
        qbias_grad,
        weight_grads[:, inner_width:edge_two],
        kbias_grad,
        weight_grads[:, edge_two:edge_three],
        vbias_grad,
        weight_grads[:, edge_four:edge_five],
        weight_grads[:, edge_three:edge_four],
        ubias_grad,
        weight_grads[:, edge_five:],
        obias_grad,
    )


def solution(mesh):
    return jax.shard_map(
        local,
        mesh=mesh,
        in_specs=(
            P("fsdp", "ctx", None),
            P("fsdp", "ctx", None),
            P("fsdp"),
            P(),
            P(),
            P(),
            P("fsdp", "tp"),
            P("tp"),
            P("fsdp", "tp"),
            P("tp"),
            P("fsdp", "tp"),
            P("tp"),
            P("fsdp", "tp"),
            P(),
            P("fsdp", "tp"),
            P("tp"),
            P("fsdp", "tp"),
            P(),
        ),
        out_specs=(
            P("fsdp", "ctx", None),
            P("fsdp", "ctx", None),
            P(),
            P(),
            P("fsdp", "tp"),
            P("tp"),
            P("fsdp", "tp"),
            P("tp"),
            P("fsdp", "tp"),
            P("tp"),
            P("fsdp", "tp"),
            P("fsdp", "tp"),
            P("tp"),
            P("fsdp", "tp"),
            P(),
        ),
        check_vma=False,
    )
```

profile of v0, /device:TPU:0, one launch (start us, length us, event | category | flops | bytes accessed | tf_op | source)
XLA Modules:
  0.0 2836.2 jit_solution(8669938643243681293)
XLA Ops:
  14.0 51.3 %all-gather.9.cloned.1.call-done = bf16[2048,1024]{1,0:T(8,128)(2,1)} async-done(((bf16[512,1024]{1,0:T(8,128)(2,1)}), bf16[2048,1024]{1,0:T(8,128)(2,1)}) %all-gather.9.cloned.1.call-update) | async-done | bytes 4194320 | tf_op jit(solution)/shard_map/all_gather | solution.py:86
  72.7 47.3 %all-gather.15.cloned.1.call-done = bf16[2048,1024]{1,0:T(8,128)(2,1)} async-done(((bf16[512,1024]{1,0:T(8,128)(2,1)}), bf16[2048,1024]{1,0:T(8,128)(2,1)}) %all-gather.15.cloned.1.call-update) | async-done | bytes 4194320 | tf_op jit(solution)/shard_map/all_gather | solution.py:85
  134.8 39.8 %all-gather.13.cloned.1.call-done = bf16[2048,1024]{1,0:T(8,128)(2,1)} async-done(((bf16[512,1024]{1,0:T(8,128)(2,1)}), bf16[2048,1024]{1,0:T(8,128)(2,1)}) %all-gather.13.cloned.1.call-update) | async-done | bytes 4194320 | tf_op jit(solution)/shard_map/all_gather | solution.py:84
  184.9 8.3 fusion.57
  210.7 18.2 all-gather.19.cloned.1.call-done
  242.1 69.7 %all-gather.11.cloned.1.call-done = bf16[2,1024,1024]{2,1,0:T(8,128)(2,1)} async-done(((bf16[2,256,1024]{2,1,0:T(8,128)(2,1)}), bf16[2,1024,1024]{2,1,0:T(8,128)(2,1)}) %all-gather.11.cloned.1.call-update) | async-done | bytes 4194320 | tf_op jit(solution)/shard_map/all_gather | solution.py:126
  318.0 74.9 %all-gather.17.cloned.1.call-done = bf16[2,1024,1024]{1,2,0:T(8,128)(2,1)} async-done(((bf16[2,256,1024]{1,2,0:T(8,128)(2,1)}), bf16[2,1024,1024]{1,2,0:T(8,128)(2,1)}) %all-gather.17.cloned.1.call-update) | async-done | bytes 4194320 | tf_op jit(solution)/shard_map/all_gather | solution.py:125
  392.9 20.1 fusion.59
  412.9 14.6 fusion
  427.5 22.3 multiply_reduce_fusion
  449.8 29.6 %multiply_convert_fusion = bf16[2,16,256,1024]{3,2,1,0:T(8,128)(2,1)} fusion(f32[2,16,256,1024]{3,2,1,0:T(8,128)} %get-tuple-element.72, f32[2,16,256,1024]{3,2,1,0:T(8,128)} %get-tuple-element.70, f32[2,16,256]{2,1,0:T(8,128)S(1)} %get-tuple-element.71, f32[2,16,256]{2,1,0:T(8,128)S(1)} %log_add_fusion), kind=kLoop, calls=%fused_computation.1 | loop fusion | flops 33554432 | bytes 83951616 | tf_op jit(solution)/shard_map/convert_element_type | solution.py:180
  479.4 12.2 broadcast_multiply_fusion
  491.6 17.0 fusion.2
  508.6 11.9 pad_maximum_fusion.1
  521.2 15.1 fusion.43
  539.9 13.7 multiply_bitcast_fusion
  554.9 14.4 fusion.61
  569.3 140.3 %all-gather.23.cloned.1.call-done = bf16[2048,4096]{1,0:T(8,128)(2,1)} async-done(((bf16[512,4096]{1,0:T(8,128)(2,1)}), bf16[2048,4096]{1,0:T(8,128)(2,1)}) %all-gather.23.cloned.1.call-update) | async-done | bytes 16777232 | tf_op jit(solution)/shard_map/all_gather | solution.py:89
  709.6 22.4 convert_reduce_fusion
  732.1 22.1 convolution_bitcast_fusion
  754.2 238.2 %reduce-scatter.3.cloned.1.call-done = f32[256,2,2048]{0,2,1:T(8,128)} async-done(((f32[1024,2,2048]{0,2,1:T(8,128)}), f32[256,2,2048]{0,2,1:T(8,128)}) %reduce-scatter.3.cloned.1.call-update) | async-done | bytes 4194320 | tf_op jit(solution)/shard_map/reduce_scatter | solution.py:196
  1008.6 26.3 fusion.13
  1034.9 65.5 %pad_maximum_fusion = f32[2048,12288]{1,0:T(8,128)} fusion(f32[2048,5120]{1,0:T(8,128)} %convolution_bitcast_fusion, f32[2048,7168]{1,0:T(8,128)} %fusion.13), kind=kLoop, calls=%fused_computation | loop fusion | flops 25165824 | bytes 201326592 | tf_op jit(solution)/shard_map/concatenate | solution.py:269
  1108.4 16.2 convolution_add_fusion
  1137.8 18.3 add_add_fusion
  1156.2 773.7 %reduce-scatter.5.cloned.1.call-done = f32[512,12288]{1,0:T(8,128)} async-done(((f32[2048,12288]{1,0:T(8,128)}), f32[512,12288]{1,0:T(8,128)}) %reduce-scatter.5.cloned.1.call-update) | async-done | bytes 25165840 | tf_op jit(solution)/shard_map/reduce_scatter | solution.py:268
  1932.8 39.2 %all-reduce.7.cloned.1.call-done = (f32[512,2048]{1,0:T(8,128)}, f32[512,2048]{1,0:T(8,128)}) async-done(((f32[512,2048]{1,0:T(8,128)}, f32[512,2048]{1,0:T(8,128)}), (f32[512,2048]{1,0:T(8,128)}, f32[512,2048]{1,0:T(8,128)})) %all-reduce.7.cloned.1.call-update) | async-done | bytes 8388624 | tf_op jit(solution)/shard_map/psum | solution.py:153
  1975.7 82.3 %all-reduce = (f32[2048]{0:T(1024)}, f32[2048]{0:T(1024)}, f32[1024]{0:T(1024)}, f32[1024]{0:T(1024)}, f32[1024]{0:T(1024)}, /*index=5*/f32[4096]{0:T(1024)}, f32[2048]{0:T(1024)}) all-reduce(f32[2048]{0:T(1024)S(1)} %get-tuple-element.15, f32[2048]{0:T(1024)S(1)} %get-tuple-element.18, ...), channel_id=1, replica_groups=mesh['fsdp'=4,'ctx'=4,'tp'=2] {'fsdp','ctx'}, use_global_device_ids=true, to_apply=%region_13.14 | all-reduce | flops 13312 | bytes 106496 | tf_op jit(solution)/shard_map/psum | solution.py:252
  2058.0 6.8 fusion.37
  2064.8 745.8 %all-reduce.5.cloned.1.call-done = f32[512,12288]{1,0:T(8,128)} async-done(((f32[512,12288]{1,0:T(8,128)}), f32[512,12288]{1,0:T(8,128)}) %all-reduce.5.cloned.1.call-update) | async-done | bytes 25165840 | tf_op jit(solution)/shard_map/psum | solution.py:271
  2810.6 7.5 fusion.56
  2818.1 11.1 fusion.55
  (182 shorter events, 125.4 us)
Async XLA Ops:
  7.2 58.1 %all-gather.9.cloned.1.call-start = ((), (), s32[]{:S(2)}) async-start(), calls=%async_computation.2 | async-start | bytes 5242880 | tf_op jit(solution)/shard_map/all_gather | solution.py:86
  8.0 112.0 %all-gather.15.cloned.1.call-start = ((), (), s32[]{:S(2)}) async-start(), calls=%async_computation.5 | async-start | bytes 5242880 | tf_op jit(solution)/shard_map/all_gather | solution.py:85
  8.7 165.8 %all-gather.13.cloned.1.call-start = ((), (), s32[]{:S(2)}) async-start(), calls=%async_computation.4 | async-start | bytes 5242880 | tf_op jit(solution)/shard_map/all_gather | solution.py:84
  9.4 219.5 %all-gather.19.cloned.1.call-start = ((), (), s32[]{:S(2)}) async-start(), calls=%async_computation.7 | async-start | bytes 5242880 | tf_op jit(solution)/shard_map/all_gather | solution.py:87
  10.0 301.7 %all-gather.11.cloned.1.call-start = ((), (), s32[]{:S(2)}) async-start(), calls=%async_computation.3 | async-start | bytes 5242880 | tf_op jit(solution)/shard_map/all_gather | solution.py:126
  14.0 57.7 %copy-start.35 = (bf16[1024]{0:T(1024)(128)(2,1)S(1)}, bf16[1024]{0:T(1024)(128)(2,1)}, u32[]{:S(2)}) copy-start(bf16[1024]{0:T(1024)(128)(2,1)} %param.25) | copy-start | bytes 6148
  14.0 57.8 %copy-start.36 = (bf16[1024]{0:T(1024)(128)(2,1)S(1)}, bf16[1024]{0:T(1024)(128)(2,1)}, u32[]{:S(2)}) copy-start(bf16[1024]{0:T(1024)(128)(2,1)} %param.27) | copy-start | bytes 6148
  14.0 57.8 %copy-start.37 = (s32[8]{0:T(128)S(1)}, s32[8]{0:T(128)}, u32[]{:S(2)}) copy-start(s32[8]{0:T(128)} %param.21) | copy-start | bytes 100
  14.0 105.9 %copy-start.3 = (bf16[512,2048]{1,0:T(8,128)(2,1)S(1)}, bf16[512,2048]{1,0:T(8,128)(2,1)}, u32[]{:S(2)}) copy-start(bf16[512,2048]{1,0:T(8,128)(2,1)} %fusion.32) | copy-start | bytes 6291460
  71.5 321.4 %all-gather.17.cloned.1.call-start = ((), (), s32[]{:S(2)}) async-start(), calls=%async_computation.6 | async-start | bytes 5242880 | tf_op jit(solution)/shard_map/all_gather | solution.py:125
  72.7 128.0 %copy-start.16 = (f32[256,16]{0,1:T(8,128)}, f32[256,16]{0,1:T(8,128)S(1)}, u32[]{:S(2)}) copy-start(f32[256,16]{0,1:T(8,128)S(1)} %get-tuple-element.68) | copy-start | bytes 49156
  204.9 350.0 %all-gather.21.cloned.1.call-start = ((), (), s32[]{:S(2)}) async-start(), calls=%async_computation.8 | async-start | bytes 20971520 | tf_op jit(solution)/shard_map/all_gather | solution.py:88
  205.7 503.9 %all-gather.23.cloned.1.call-start = ((), (), s32[]{:S(2)}) async-start(), calls=%async_computation.9 | async-start | bytes 20971520 | tf_op jit(solution)/shard_map/all_gather | solution.py:89
  206.4 785.9 %reduce-scatter.3.cloned.1.call-start = ((), (), s32[]{:S(2)}) async-start(), calls=%async_computation.10 | async-start | bytes 20971520 | tf_op jit(solution)/shard_map/reduce_scatter | solution.py:196
  242.1 150.8 %copy-start.7 = (bf16[2,256,16,32]{1,3,2,0:T(8,128)(2,1)S(1)}, bf16[2,256,16,32]{1,3,2,0:T(8,128)(2,1)}, u32[]{:S(2)}) copy-start(bf16[2,256,16,32]{1,3,2,0:T(8,128)(2,1)} %copy.99) | copy-start | bytes 1572868
  242.1 150.8 %copy-start.8 = (pred[2,256,1024]{2,1,0:T(8,128)(4,1)S(1)}, pred[2,256,1024]{2,1,0:T(8,128)(4,1)}, u32[]{:S(2)}) copy-start(pred[2,256,1024]{2,1,0:T(8,128)(4,1)} %broadcast_or_fusion) | copy-start | bytes 1572868
  242.1 150.8 %copy-start.14 = (bf16[2,256,16,16]{1,3,2,0:T(8,128)(2,1)S(1)}, bf16[2,256,16,16]{1,3,2,0:T(8,128)(2,1)}, u32[]{:S(2)}) copy-start(bf16[2,256,16,16]{1,3,2,0:T(8,128)(2,1)} %get-tuple-element.57) | copy-start | bytes 786436
  412.9 14.6 copy-start.2
  520.5 1409.4 %reduce-scatter.5.cloned.1.call-start = ((), (), s32[]{:S(2)}) async-start(), calls=%async_computation.11 | async-start | bytes 125829120 | tf_op jit(solution)/shard_map/reduce_scatter | solution.py:268
  539.9 15.0 copy-start.4
  754.1 242.3 %copy-start.17 = (f32[256,16]{0,1:T(8,128)S(1)}, f32[256,16]{0,1:T(8,128)}, u32[]{:S(2)}) copy-start(f32[256,16]{0,1:T(8,128)} %copy-done.16) | copy-start | bytes 49156
  754.1 242.3 %copy-start.20 = (f32[256,16]{0,1:T(8,128)S(1)}, f32[256,16]{0,1:T(8,128)}, u32[]{:S(2)}) copy-start(f32[256,16]{0,1:T(8,128)} %get-tuple-element.66) | copy-start | bytes 49156
  1100.5 871.5 %all-reduce.7.cloned.1.call-start = ((), (), s32[]{:S(2)}) async-start(), calls=%async_computation.13 | async-start | bytes 16777216 | tf_op jit(solution)/shard_map/psum | solution.py:153
  1108.4 16.2 copy-start.12
  1108.4 16.2 copy-start.40
  1156.2 1654.4 %all-reduce.5.cloned.1.call-start = ((), (), s32[]{:S(2)}) async-start(), calls=%async_computation.12 | async-start | bytes 50331648 | tf_op jit(solution)/shard_map/psum | solution.py:271
  1929.9 42.1 %copy-start.1 = (bf16[2,256,2048]{2,1,0:T(8,128)(2,1)S(1)}, bf16[2,256,2048]{2,1,0:T(8,128)(2,1)}, u32[]{:S(2)}) copy-start(bf16[2,256,2048]{2,1,0:T(8,128)(2,1)} %param.18) | copy-start | bytes 6291460
  1929.9 42.1 %copy-start.19 = (f32[2048]{0:T(1024)S(1)}, f32[2048]{0:T(1024)}, u32[]{:S(2)}) copy-start(f32[2048]{0:T(1024)} %copy-done.18) | copy-start | bytes 24580
  1929.9 42.1 %copy-start.22 = (f32[1,2,2,128]{3,1,2,0:T(2,128)S(1)}, f32[1,2,2,128]{3,1,2,0:T(2,128)}, u32[]{:S(2)}) copy-start(f32[1,2,2,128]{3,1,2,0:T(2,128)} %copy-done.21) | copy-start | bytes 6148
  1929.9 42.0 %copy-start.24 = (f32[1,2,2,128]{3,1,2,0:T(2,128)S(1)}, f32[1,2,2,128]{3,1,2,0:T(2,128)}, u32[]{:S(2)}) copy-start(f32[1,2,2,128]{3,1,2,0:T(2,128)} %copy-done.23) | copy-start | bytes 6148
  1930.6 45.0 %copy-start.27 = (f32[4096]{0:T(1024)S(1)}, f32[4096]{0:T(1024)}, u32[]{:S(2)}) copy-start(f32[4096]{0:T(1024)} %get-tuple-element.28) | copy-start | bytes 49156
  1930.6 45.0 %copy-start.28 = (f32[1024]{0:T(1024)S(1)}, f32[1024]{0:T(1024)}, u32[]{:S(2)}) copy-start(f32[1024]{0:T(1024)} %get-tuple-element.30) | copy-start | bytes 12292
  (22 other events, 61.9 us)
Sparse Core Ops, SparseCore 0:
  9.9 55.3 all-gather.8
  67.2 52.6 all-gather.14
  121.8 52.6 all-gather.12
  176.2 52.6 all-gather.18
  230.9 80.7 all-gather.10
  313.7 79.0 all-gather.16
  394.7 155.5 all-gather.20
  552.2 157.4 all-gather.22
  712.0 280.2 reduce-scatter.2
  1100.6 829.2 reduce-scatter.4
  1933.0 38.8 all-reduce.6
  1974.3 836.1 all-reduce.4
where the time goes:
time: 2840 us
  waiting for transfers between devices  2240 us (79%)
  matrix products  263 us (9%)
  other arithmetic  148 us (5%)
  local copies, waits for them, and re-layouts  84.7 us (3%)
  blocking collectives  82.3 us (3%)
    reduce_scatter x1, waiting for transfers between devices, local(): lax.psum_scatter(jnp.concatenate([left_part, right_part], axis=1), 'fsdp'...  774 us
    psum x1, waiting for transfers between devices, local(): weight_grads = lax.psum(scattered, 'ctx')  746 us
    reduce_scatter x1, waiting for transfers between devices, local(): lax.psum_scatter(jnp.concatenate([grad_key_part.reshape(row_count, seq_co...  238 us
    all_gather x1, waiting for transfers between devices, local(): lax.all_gather(down_weight, 'fsdp', axis=0, tiled=True)  140 us
    psum x1, blocking collectives, local(): lax.psum((small_terms[0], small_terms[1], small_terms[2], small_terms[3],...  82.3 us
    all_gather x1, waiting for transfers between devices, local(): lax.all_gather(key_rot, 'ctx', axis=1, tiled=True)  74.9 us
    all_gather x1, waiting for transfers between devices, local(): lax.all_gather(value_rows, 'ctx', axis=1, tiled=True)  69.7 us
    concatenate x1, other arithmetic, local(): jnp.concatenate([left_part, right_part], axis=1)  65.5 us
  transfers between devices with their start and end apart: 12, of which 11 were waited for; matrix products, arithmetic and copies ran while one was open for 13% of the time, Pallas kernels for 0%

commit v1 on v0

--- a/solution.py
+++ b/solution.py
@@ -8,6 +8,28 @@
 SEQ_LEN = 1024
 masked_fill = -1e30
 norm_eps = 1e-05
+
+
+def in_order(parts, dim):
+    shape = list(parts.shape[1:])
+    shape[dim] *= parts.shape[0]
+    return jnp.moveaxis(parts, 0, dim).reshape(shape)
+
+
+def collect(x, axis, dim):
+    peers = lax.axis_size(axis)
+    pairs = [(i, (i + 1) % peers) for i in range(peers)]
+    back = [(b, a) for a, b in pairs]
+    lower, upper = ([], [])
+    for step in range(peers - 1):
+        if step % 2 == 0:
+            lower.append(lax.ppermute(lower[-1] if lower else x, axis, pairs))
+        else:
+            upper.append(lax.ppermute(upper[-1] if upper else x, axis, back))
+    tiles = jnp.stack([*lower[::-1], x, *upper])
+    shift = lax.axis_index(axis) - len(lower)
+    tiles = tiles[(jnp.arange(peers) - shift) % peers]
+    return in_order(tiles, dim)
 
 
 def positions(group_order, row_start, row_count, group_len):
@@ -123,7 +145,7 @@
     )
     keys_all, values_all = (
         lax.all_gather(key_rot, "ctx", axis=1, tiled=True),
-        lax.all_gather(value_rows, "ctx", axis=1, tiled=True),
+        collect(value_rows, "ctx", 1),
     )
 
     def scores_for(key_block):

time: 2840 us -> 2840 us (level)
  waiting for transfers between devices: 2240 us -> 2210 us
    all_gather x1, waiting for transfers between devices: 140 us -> 41.6 us  [local(): lax.all_gather(down_weight, 'fsdp', axis=0, tiled=True)]
    ppermute x0 -> x3, waiting for transfers between devices: none -> 68.2 us  [the longest x2 48.5 us: collect(): lower.append(lax.ppermute(lower[-1] if lower else x, axis, pairs))]
  transfers between devices with their start and end apart: 12 -> 15, of which waited for: 11 -> 14; matrix products, arithmetic and copies ran while one was open for 13% -> 14% of each run, Pallas kernels for 0% -> 0%
where the time goes in v1:
time: 2840 us
  waiting for transfers between devices  2210 us (78%)
  matrix products  265 us (9%)
  other arithmetic  152 us (5%)
  local copies, waits for them, and re-layouts  105 us (4%)
  blocking collectives  82.3 us (3%)
    reduce_scatter x1, waiting for transfers between devices, local(): lax.psum_scatter(jnp.concatenate([left_part, right_part], axis=1), 'fsdp'...  774 us
    psum x1, waiting for transfers between devices, local(): weight_grads = lax.psum(scattered, 'ctx')  746 us
    reduce_scatter x1, waiting for transfers between devices, local(): lax.psum_scatter(jnp.concatenate([grad_key_part.reshape(row_count, seq_co...  238 us
    psum x1, blocking collectives, local(): lax.psum((small_terms[0], small_terms[1], small_terms[2], small_terms[3],...  82.3 us
    all_gather x1, waiting for transfers between devices, local(): lax.all_gather(key_rot, 'ctx', axis=1, tiled=True)  74.9 us
    all_gather x1, waiting for transfers between devices, local(): lax.all_gather(value_rows, 'ctx', axis=1, tiled=True)  69.7 us
    concatenate x1, other arithmetic, local(): jnp.concatenate([left_part, right_part], axis=1)  65.5 us
  transfers between devices with their start and end apart: 15, of which 14 were waited for; matrix products, arithmetic and copies ran while one was open for 14% of the time, Pallas kernels for 0%

profile of v1, /device:TPU:0, one launch (start us, length us, event | category | flops | bytes accessed | tf_op | source)
XLA Modules:
  0.0 2836.2 jit_solution(17949404115226587864)
XLA Ops:
  14.0 51.3 %all-gather.9.cloned.1.call-done = bf16[2048,1024]{1,0:T(8,128)(2,1)} async-done(((bf16[512,1024]{1,0:T(8,128)(2,1)}), bf16[2048,1024]{1,0:T(8,128)(2,1)}) %all-gather.9.cloned.1.call-update) | async-done | bytes 4194320 | tf_op jit(solution)/shard_map/all_gather | solution.py:108
  72.7 47.3 %all-gather.13.cloned.1.call-done = bf16[2048,1024]{1,0:T(8,128)(2,1)} async-done(((bf16[512,1024]{1,0:T(8,128)(2,1)}), bf16[2048,1024]{1,0:T(8,128)(2,1)}) %all-gather.13.cloned.1.call-update) | async-done | bytes 4194320 | tf_op jit(solution)/shard_map/all_gather | solution.py:107
  134.8 39.8 %all-gather.11.cloned.1.call-done = bf16[2048,1024]{1,0:T(8,128)(2,1)} async-done(((bf16[512,1024]{1,0:T(8,128)(2,1)}), bf16[2048,1024]{1,0:T(8,128)(2,1)}) %all-gather.11.cloned.1.call-update) | async-done | bytes 4194320 | tf_op jit(solution)/shard_map/all_gather | solution.py:106
  210.7 18.2 all-gather.17.cloned.1.call-done
  242.1 69.7 %all-gather.23.cloned.1.call-done = bf16[2,1024,1024]{2,1,0:T(8,128)(2,1)} async-done(((bf16[2,256,1024]{2,1,0:T(8,128)(2,1)}), bf16[2,1024,1024]{2,1,0:T(8,128)(2,1)}) %all-gather.23.cloned.1.call-update) | async-done | bytes 4194320 | tf_op jit(solution)/shard_map/all_gather | solution.py:188
  317.9 74.9 %all-gather.15.cloned.1.call-done = bf16[2,1024,1024]{1,2,0:T(8,128)(2,1)} async-done(((bf16[2,256,1024]{1,2,0:T(8,128)(2,1)}), bf16[2,1024,1024]{1,2,0:T(8,128)(2,1)}) %all-gather.15.cloned.1.call-update) | async-done | bytes 4194320 | tf_op jit(solution)/shard_map/all_gather | solution.py:147
  392.9 20.1 fusion.61
  412.9 14.6 fusion
  427.5 22.3 multiply_reduce_fusion
  449.8 29.6 %multiply_convert_fusion = bf16[2,16,256,1024]{3,2,1,0:T(8,128)(2,1)} fusion(f32[2,16,256,1024]{3,2,1,0:T(8,128)} %get-tuple-element.72, f32[2,16,256,1024]{3,2,1,0:T(8,128)} %get-tuple-element.70, f32[2,16,256]{2,1,0:T(8,128)S(1)} %get-tuple-element.71, f32[2,16,256]{2,1,0:T(8,128)S(1)} %log_add_fusion), kind=kLoop, calls=%fused_computation.2 | loop fusion | flops 33554432 | bytes 83951616 | tf_op jit(solution)/shard_map/convert_element_type | solution.py:202
  479.4 12.2 broadcast_multiply_fusion
  491.6 17.0 fusion.2
  508.6 11.9 pad_maximum_fusion.1
  525.5 24.0 collective-permute-done
  549.6 19.7 collective-permute-done.2
  569.3 24.4 collective-permute-done.1
  617.3 17.4 fusion.43
  638.3 13.7 multiply_bitcast_fusion
  653.4 14.6 fusion.63
  668.0 41.6 %all-gather.21.cloned.1.call-done = bf16[2048,4096]{1,0:T(8,128)(2,1)} async-done(((bf16[512,4096]{1,0:T(8,128)(2,1)}), bf16[2048,4096]{1,0:T(8,128)(2,1)}) %all-gather.21.cloned.1.call-update) | async-done | bytes 16777232 | tf_op jit(solution)/shard_map/all_gather | solution.py:111
  709.6 22.0 convert_reduce_fusion
  731.7 22.3 convolution_bitcast_fusion
  754.0 238.3 %reduce-scatter.3.cloned.1.call-done = f32[256,2,2048]{0,2,1:T(8,128)} async-done(((f32[1024,2,2048]{0,2,1:T(8,128)}), f32[256,2,2048]{0,2,1:T(8,128)}) %reduce-scatter.3.cloned.1.call-update) | async-done | bytes 4194320 | tf_op jit(solution)/shard_map/reduce_scatter | solution.py:218
  1008.6 26.2 fusion.13
  1034.8 65.5 %pad_maximum_fusion = f32[2048,12288]{1,0:T(8,128)} fusion(f32[2048,5120]{1,0:T(8,128)} %convolution_bitcast_fusion, f32[2048,7168]{1,0:T(8,128)} %fusion.13), kind=kLoop, calls=%fused_computation.1 | loop fusion | flops 25165824 | bytes 201326592 | tf_op jit(solution)/shard_map/concatenate | solution.py:291
  1108.3 16.2 convolution_add_fusion
  1137.7 18.3 add_add_fusion
  1156.1 773.8 %reduce-scatter.5.cloned.1.call-done = f32[512,12288]{1,0:T(8,128)} async-done(((f32[2048,12288]{1,0:T(8,128)}), f32[512,12288]{1,0:T(8,128)}) %reduce-scatter.5.cloned.1.call-update) | async-done | bytes 25165840 | tf_op jit(solution)/shard_map/reduce_scatter | solution.py:290
  1932.8 39.2 %all-reduce.7.cloned.1.call-done = (f32[512,2048]{1,0:T(8,128)}, f32[512,2048]{1,0:T(8,128)}) async-done(((f32[512,2048]{1,0:T(8,128)}, f32[512,2048]{1,0:T(8,128)}), (f32[512,2048]{1,0:T(8,128)}, f32[512,2048]{1,0:T(8,128)})) %all-reduce.7.cloned.1.call-update) | async-done | bytes 8388624 | tf_op jit(solution)/shard_map/psum | solution.py:175
  1975.6 82.3 %all-reduce = (f32[2048]{0:T(1024)}, f32[2048]{0:T(1024)}, f32[1024]{0:T(1024)}, f32[1024]{0:T(1024)}, f32[1024]{0:T(1024)}, /*index=5*/f32[4096]{0:T(1024)}, f32[2048]{0:T(1024)}) all-reduce(f32[2048]{0:T(1024)S(1)} %get-tuple-element.15, f32[2048]{0:T(1024)S(1)} %get-tuple-element.18, ...), channel_id=1, replica_groups=mesh['fsdp'=4,'ctx'=4,'tp'=2] {'fsdp','ctx'}, use_global_device_ids=true, to_apply=%region_13.14 | all-reduce | flops 13312 | bytes 106496 | tf_op jit(solution)/shard_map/psum | solution.py:274
  2064.7 745.8 %all-reduce.5.cloned.1.call-done = f32[512,12288]{1,0:T(8,128)} async-done(((f32[512,12288]{1,0:T(8,128)}), f32[512,12288]{1,0:T(8,128)}) %all-reduce.5.cloned.1.call-update) | async-done | bytes 25165840 | tf_op jit(solution)/shard_map/psum | solution.py:293
  2818.1 11.1 fusion.57
  (196 shorter events, 175.7 us)
Async XLA Ops:
  7.2 58.1 %all-gather.9.cloned.1.call-start = ((), (), s32[]{:S(2)}) async-start(), calls=%async_computation.2 | async-start | bytes 5242880 | tf_op jit(solution)/shard_map/all_gather | solution.py:108
  8.0 112.0 %all-gather.13.cloned.1.call-start = ((), (), s32[]{:S(2)}) async-start(), calls=%async_computation.4 | async-start | bytes 5242880 | tf_op jit(solution)/shard_map/all_gather | solution.py:107
  8.7 165.8 %all-gather.11.cloned.1.call-start = ((), (), s32[]{:S(2)}) async-start(), calls=%async_computation.3 | async-start | bytes 5242880 | tf_op jit(solution)/shard_map/all_gather | solution.py:106
  9.4 219.5 %all-gather.17.cloned.1.call-start = ((), (), s32[]{:S(2)}) async-start(), calls=%async_computation.6 | async-start | bytes 5242880 | tf_op jit(solution)/shard_map/all_gather | solution.py:109
  10.0 301.7 %all-gather.23.cloned.1.call-start = ((), (), s32[]{:S(2)}) async-start(), calls=%async_computation.9 | async-start | bytes 5242880 | tf_op jit(solution)/shard_map/all_gather | solution.py:188
  14.0 57.7 %copy-start.36 = (bf16[1024]{0:T(1024)(128)(2,1)S(1)}, bf16[1024]{0:T(1024)(128)(2,1)}, u32[]{:S(2)}) copy-start(bf16[1024]{0:T(1024)(128)(2,1)} %param.25) | copy-start | bytes 6148
  14.0 57.8 %copy-start.37 = (bf16[1024]{0:T(1024)(128)(2,1)S(1)}, bf16[1024]{0:T(1024)(128)(2,1)}, u32[]{:S(2)}) copy-start(bf16[1024]{0:T(1024)(128)(2,1)} %param.27) | copy-start | bytes 6148
  14.0 57.8 %copy-start.38 = (s32[8]{0:T(128)S(1)}, s32[8]{0:T(128)}, u32[]{:S(2)}) copy-start(s32[8]{0:T(128)} %param.21) | copy-start | bytes 100
  14.0 105.9 %copy-start.3 = (bf16[512,2048]{1,0:T(8,128)(2,1)S(1)}, bf16[512,2048]{1,0:T(8,128)(2,1)}, u32[]{:S(2)}) copy-start(bf16[512,2048]{1,0:T(8,128)(2,1)} %fusion.32) | copy-start | bytes 6291460
  71.5 321.4 %all-gather.15.cloned.1.call-start = ((), (), s32[]{:S(2)}) async-start(), calls=%async_computation.5 | async-start | bytes 5242880 | tf_op jit(solution)/shard_map/all_gather | solution.py:147
  72.7 128.0 %copy-start.17 = (f32[256,16]{0,1:T(8,128)}, f32[256,16]{0,1:T(8,128)S(1)}, u32[]{:S(2)}) copy-start(f32[256,16]{0,1:T(8,128)S(1)} %get-tuple-element.68) | copy-start | bytes 49156
  204.9 448.4 %all-gather.19.cloned.1.call-start = ((), (), s32[]{:S(2)}) async-start(), calls=%async_computation.7 | async-start | bytes 20971520 | tf_op jit(solution)/shard_map/all_gather | solution.py:110
  205.7 503.9 %all-gather.21.cloned.1.call-start = ((), (), s32[]{:S(2)}) async-start(), calls=%async_computation.8 | async-start | bytes 20971520 | tf_op jit(solution)/shard_map/all_gather | solution.py:111
  206.4 785.9 %reduce-scatter.3.cloned.1.call-start = ((), (), s32[]{:S(2)}) async-start(), calls=%async_computation.10 | async-start | bytes 20971520 | tf_op jit(solution)/shard_map/reduce_scatter | solution.py:218
  242.1 150.8 %copy-start.7 = (bf16[2,256,16,32]{1,3,2,0:T(8,128)(2,1)S(1)}, bf16[2,256,16,32]{1,3,2,0:T(8,128)(2,1)}, u32[]{:S(2)}) copy-start(bf16[2,256,16,32]{1,3,2,0:T(8,128)(2,1)} %copy.102) | copy-start | bytes 1572868
  242.1 150.8 %copy-start.8 = (pred[2,256,1024]{2,1,0:T(8,128)(4,1)S(1)}, pred[2,256,1024]{2,1,0:T(8,128)(4,1)}, u32[]{:S(2)}) copy-start(pred[2,256,1024]{2,1,0:T(8,128)(4,1)} %broadcast_or_fusion) | copy-start | bytes 1572868
  242.1 150.8 %copy-start.15 = (bf16[2,256,16,16]{1,3,2,0:T(8,128)(2,1)S(1)}, bf16[2,256,16,16]{1,3,2,0:T(8,128)(2,1)}, u32[]{:S(2)}) copy-start(bf16[2,256,16,16]{1,3,2,0:T(8,128)(2,1)} %get-tuple-element.57) | copy-start | bytes 786436
  520.5 29.1 %copy-start.30 = (bf16[4096]{0:T(1024)(128)(2,1)S(1)}, bf16[4096]{0:T(1024)(128)(2,1)}, u32[]{:S(2)}) copy-start(bf16[4096]{0:T(1024)(128)(2,1)} %param.33) | copy-start | bytes 24580
  520.5 1409.4 %reduce-scatter.5.cloned.1.call-start = ((), (), s32[]{:S(2)}) async-start(), calls=%async_computation.11 | async-start | bytes 125829120 | tf_op jit(solution)/shard_map/reduce_scatter | solution.py:290
  521.7 27.9 collective-permute-start
  521.7 47.6 %collective-permute-start.2 = (bf16[2,256,1024]{2,1,0:T(8,128)(2,1)S(1)}, bf16[2,256,1024]{2,1,0:T(8,128)(2,1)S(1)}, u32[]{:S(2)}, u32[]{:S(2)}) collective-permute-start(bf16[2,256,1024]{2,1,0:T(8,128)(2,1)S(1)} %bitcast.149), channel_id=1, source_target_pairs={{2,0},{4,2},{6,4},{0,6},{3,1},{5,3},{7,5},{1,7},{10,8},{12,10},{14... | collective-permute-start | bytes 3145736 | tf_op jit(solution)/shard_map/ppermute | solution.py:28
  549.5 44.2 %collective-permute-start.1 = (bf16[2,256,1024]{2,1,0:T(8,128)(2,1)S(1)}, bf16[2,256,1024]{2,1,0:T(8,128)(2,1)}, u32[]{:S(2)}, u32[]{:S(2)}) collective-permute-start(bf16[2,256,1024]{2,1,0:T(8,128)(2,1)S(1)} %collective-permute-done), channel_id=1, source_target_pairs={{0,2},{2,4},{4,6},{6,0},{1,3},{3,5},{5,7},{7,1},{8,10},{10,12},{12... | collective-permute-start | bytes 3145736 | tf_op jit(solution)/shard_map/ppermute | solution.py:26
  754.0 242.5 %copy-start.18 = (f32[256,16]{0,1:T(8,128)S(1)}, f32[256,16]{0,1:T(8,128)}, u32[]{:S(2)}) copy-start(f32[256,16]{0,1:T(8,128)} %copy-done.17) | copy-start | bytes 49156
  754.0 242.5 %copy-start.21 = (f32[256,16]{0,1:T(8,128)S(1)}, f32[256,16]{0,1:T(8,128)}, u32[]{:S(2)}) copy-start(f32[256,16]{0,1:T(8,128)} %get-tuple-element.66) | copy-start | bytes 49156
  1100.4 871.6 %all-reduce.7.cloned.1.call-start = ((), (), s32[]{:S(2)}) async-start(), calls=%async_computation.13 | async-start | bytes 16777216 | tf_op jit(solution)/shard_map/psum | solution.py:175
  1156.1 1654.5 %all-reduce.5.cloned.1.call-start = ((), (), s32[]{:S(2)}) async-start(), calls=%async_computation.12 | async-start | bytes 50331648 | tf_op jit(solution)/shard_map/psum | solution.py:293
  1929.9 42.1 %copy-start.1 = (bf16[2,256,2048]{2,1,0:T(8,128)(2,1)S(1)}, bf16[2,256,2048]{2,1,0:T(8,128)(2,1)}, u32[]{:S(2)}) copy-start(bf16[2,256,2048]{2,1,0:T(8,128)(2,1)} %param.18) | copy-start | bytes 6291460
  1929.9 42.0 %copy-start.20 = (f32[2048]{0:T(1024)S(1)}, f32[2048]{0:T(1024)}, u32[]{:S(2)}) copy-start(f32[2048]{0:T(1024)} %copy-done.19) | copy-start | bytes 24580
  1929.9 42.0 %copy-start.23 = (f32[1,2,2,128]{3,1,2,0:T(2,128)S(1)}, f32[1,2,2,128]{3,1,2,0:T(2,128)}, u32[]{:S(2)}) copy-start(f32[1,2,2,128]{3,1,2,0:T(2,128)} %copy-done.22) | copy-start | bytes 6148
  1929.9 42.0 %copy-start.25 = (f32[1,2,2,128]{3,1,2,0:T(2,128)S(1)}, f32[1,2,2,128]{3,1,2,0:T(2,128)}, u32[]{:S(2)}) copy-start(f32[1,2,2,128]{3,1,2,0:T(2,128)} %copy-done.24) | copy-start | bytes 6148
  1930.6 45.0 %copy-start.28 = (f32[4096]{0:T(1024)S(1)}, f32[4096]{0:T(1024)}, u32[]{:S(2)}) copy-start(f32[4096]{0:T(1024)} %get-tuple-element.28) | copy-start | bytes 49156
  1930.6 45.0 %copy-start.29 = (f32[1024]{0:T(1024)S(1)}, f32[1024]{0:T(1024)}, u32[]{:S(2)}) copy-start(f32[1024]{0:T(1024)} %get-tuple-element.30) | copy-start | bytes 12292
  (26 other events, 124.5 us)
Sparse Core Ops, SparseCore 0:
  9.9 55.3 all-gather.8
  67.2 52.6 all-gather.12
  121.8 52.6 all-gather.10
  176.2 52.6 all-gather.16
  230.9 80.7 all-gather.22
  313.7 79.0 all-gather.14
  394.7 155.5 all-gather.18
  552.2 157.4 all-gather.20
  712.0 280.2 reduce-scatter.2
  1100.5 829.3 reduce-scatter.4
  1933.0 38.8 all-reduce.6
  1974.3 836.1 all-reduce.4
